TPU v7x, 32 devices: a whole 2x2x4 slice. The times are simulated.
32 devices in a mesh: grp: 8 (over z, core), swap: 4 (over y, x).
Axes of the slice: x: 2, y: 2, z: 4, core: 2. Of those that a mesh axis runs over, the one named last changes fastest.
Arguments:
- amplitudes: float32 [2, 8, 4, 4, 4, 8, 8, 128], P(None, 'grp', 'swap'), may hold values from -6 to 6
- low_gates: float32 [3, 2, 128, 128], replicated, may hold values from -0.375 to 0.375
- mid_gates: float32 [2, 2, 128, 128], replicated, may hold values from -0.375 to 0.375
- pair_gate: float32 [2, 2, 2], replicated, may hold values from -3 to 3
- slice_bits: int32 [13], replicated, may hold values from 0 to 1
- phase_angles: float32 [13, 128], replicated, may hold values from -3.140625 to 3.140625
Outputs:
- final_state: float32 [2, 8, 4, 4, 4, 8, 8, 128], P(None, 'grp', 'swap')
All inputs are finite; a program needn't handle non-finite values.
Results may differ from a plain program's by a relative error of at most 0.00007.
Values sent between devices are 32-bit elements; how exact they have to be, the bound alone decides.
A program may use at most 64 MiB of HBM per device.

v0:
```python
import jax
import jax.numpy as jnp
from jax import lax
from jax.sharding import PartitionSpec as P

highest = lax.Precision.HIGHEST


def swapped(value, axis, distance):
    mask = 2**distance
    pairs = [(source, source ^ mask) for source in range(lax.axis_size(axis))]
    return lax.ppermute(value, axis, pairs)


def low_gate(psi_block, matrix):
    real_part = jnp.einsum(
        "...k,ik->...i",
        psi_block[0],
        matrix[0],
        precision=highest,
        preferred_element_type=jnp.float32,
    ) - jnp.einsum(
        "...k,ik->...i",
        psi_block[1],
        matrix[1],
        precision=highest,
        preferred_element_type=jnp.float32,
    )
    imag_part = jnp.einsum(
        "...k,ik->...i",
        psi_block[1],
        matrix[0],
        precision=highest,
        preferred_element_type=jnp.float32,
    ) + jnp.einsum(
        "...k,ik->...i",
        psi_block[0],
        matrix[1],
        precision=highest,
        preferred_element_type=jnp.float32,
    )
    return jnp.stack([real_part, imag_part])


def mid_gate(psi_block, matrix):
    shape_now = psi_block.shape
    order = matrix.shape[1]
    flat = psi_block.reshape(2, order, -1)
    real_part = jnp.dot(
        matrix[0], flat[0], precision=highest, preferred_element_type=jnp.float32
    ) - jnp.dot(matrix[1], flat[1], precision=highest, preferred_element_type=jnp.float32)
    imag_part = jnp.dot(
        matrix[0], flat[1], precision=highest, preferred_element_type=jnp.float32
    ) + jnp.dot(matrix[1], flat[0], precision=highest, preferred_element_type=jnp.float32)
    return jnp.stack([real_part, imag_part]).reshape(shape_now)


def apply_row(pair_gate, target, lower, upper):
    real_part = (
        pair_gate[0, target, 0] * lower[0]
        - pair_gate[1, target, 0] * lower[1]
        + (pair_gate[0, target, 1] * upper[0] - pair_gate[1, target, 1] * upper[1])
    )
    imag_part = (
        pair_gate[0, target, 0] * lower[1]
        + pair_gate[1, target, 0] * lower[0]
        + (pair_gate[0, target, 1] * upper[1] + pair_gate[1, target, 1] * upper[0])
    )
    return jnp.stack([real_part, imag_part])


def local(amplitudes, low_gates, mid_gates, pair_gate, slice_bits, phase_angles):
    current = amplitudes[:, 0, 0]
    theta = jnp.dot(
        slice_bits.astype(jnp.float32),
        phase_angles,
        precision=highest,
        preferred_element_type=jnp.float32,
    )
    cosine = jnp.cos(theta)
    sine = jnp.sin(theta)
    current = jnp.stack(
        [current[0] * cosine - current[1] * sine, current[0] * sine + current[1] * cosine]
    )
    current = low_gate(current, low_gates[0])
    current = mid_gate(current, mid_gates[0])
    current = low_gate(current, low_gates[1])
    top_bit = lax.axis_size("grp").bit_length() - 2
    parity = lax.axis_index("grp") // (1 << top_bit) % 2
    partner_amp = swapped(current, "grp", top_bit)
    lower_amp = jnp.where(parity == 0, current, partner_amp)
    upper_amp = jnp.where(parity == 0, partner_amp, current)
    current = jnp.where(
        parity == 0,
        apply_row(pair_gate, 0, lower_amp, upper_amp),
        apply_row(pair_gate, 1, lower_amp, upper_amp),
    )
    current = low_gate(
        mid_gate(
            lax.all_to_all(current, "swap", split_axis=1, concat_axis=1, tiled=True), mid_gates[1]
        ),
        low_gates[2],
    )
    return current[:, None, None]


def solution(mesh):
    return jax.shard_map(
        local,
        mesh=mesh,
        in_specs=(P(None, "grp", "swap", None, None, None, None, None), P(), P(), P(), P(), P()),
        out_specs=P(None, "grp", "swap", None, None, None, None, None),
        check_vma=False,
    )
```

profile of v0, /device:TPU:0, one launch (start us, length us, event | category | flops | bytes accessed | tf_op | source)
XLA Modules:
  0.0 95.3 jit_solution(15413586386958956573)
XLA Ops:
  0.0 0.7 copy-done
  0.7 0.8 fusion.82
  1.5 1.8 %fusion.24 = f32[4,4,8,8,128]{4,3,2,1,0:T(8,128)S(1)} fusion(f32[2,1,1,4,4,8,8,128]{7,6,5,4,3,2,1,0:T(8,128)} %param.6, f32[128]{0:T(128)S(1)} %get-tuple-element.22, f32[128]{0:T(128)S(1)} %get-tuple-element.21, f32[3,2,128,128]{3,2,1,0:T(8,128)} %param.7), kind=kOutput, calls=%fused_computation.38 | convolution fusion | flops 201719808 | bytes 1639424 | tf_op jit(solution)/shard_map/...k,ik->...i/dot_general | solution.py:16
  3.3 1.5 %fusion.20 = f32[4,4,8,8,128]{4,3,2,1,0:T(8,128)S(1)} fusion(f32[2,1,1,4,4,8,8,128]{7,6,5,4,3,2,1,0:T(8,128)S(1)} %copy-done.1, f32[128]{0:T(128)S(1)} %get-tuple-element.22, f32[128]{0:T(128)S(1)} %get-tuple-element.21, f32[3,2,128,128]{3,2,1,0:T(8,128)} %param.7), kind=kOutput, calls=%fused_computation.34 | convolution fusion | flops 201719808 | bytes 1639424 | tf_op jit(solution)/shard_map/...k,ik->...i/dot_general | solution.py:29
  4.9 0.6 convolution_subtract_fusion.4
  5.5 0.6 convolution_add_fusion.4
  6.4 1.0 %fusion.18 = f32[1024,128]{1,0:T(8,128)S(1)} fusion(f32[16,8,8,128]{3,2,1,0:T(8,128)S(1)} %bitcast.178, f32[2,2,128,128]{3,2,1,0:T(8,128)S(1)} %copy-done.3), kind=kOutput, calls=%fused_computation.32 | convolution fusion | flops 201326592 | bytes 1114112 | tf_op jit(solution)/shard_map/dot_general | solution.py:49
  7.4 1.0 %fusion.14 = f32[1024,128]{1,0:T(8,128)S(1)} fusion(f32[16,8,8,128]{3,2,1,0:T(8,128)S(1)} %bitcast.182, f32[2,2,128,128]{3,2,1,0:T(8,128)S(1)} %copy-done.3), kind=kOutput, calls=%fused_computation.28 | convolution fusion | flops 201326592 | bytes 1114112 | tf_op jit(solution)/shard_map/dot_general | solution.py:52
  8.4 1.0 %fusion.7 = f32[128,1024]{0,1:T(8,128)S(1)} fusion(f32[1024,128]{1,0:T(8,128)S(1)} %fusion.18, f32[16,8,8,128]{3,2,1,0:T(8,128)S(1)} %bitcast.183, f32[2,2,128,128]{3,2,1,0:T(8,128)S(1)} %copy-done.3), kind=kOutput, calls=%fused_computation.15 | convolution fusion | flops 201457664 | bytes 1638400 | tf_op jit(solution)/shard_map/dot_general | solution.py:51
  10.3 1.0 %fusion.6 = f32[128,1024]{0,1:T(8,128)S(1)} fusion(f32[1024,128]{1,0:T(8,128)S(1)} %fusion.14, f32[16,8,8,128]{3,2,1,0:T(8,128)S(1)} %bitcast.179, f32[2,2,128,128]{3,2,1,0:T(8,128)S(1)} %copy-done.3), kind=kOutput, calls=%fused_computation.13 | convolution fusion | flops 201457664 | bytes 1638400 | tf_op jit(solution)/shard_map/dot_general | solution.py:54
  13.4 1.0 %pad_maximum_fusion = f32[2,4,4,8,8,128]{5,4,3,2,1,0:T(8,128)} fusion(f32[1,4,4,8,8,128]{5,4,3,2,1,0:T(8,128)S(1)} %fusion.4, f32[1,4,4,8,8,128]{5,4,3,2,1,0:T(8,128)S(1)} %fusion.5), kind=kLoop, calls=%fused_computation.19 | loop fusion | flops 262144 | bytes 2097152 | tf_op jit(solution)/shard_map/stack | solution.py:42
  14.4 4.1 %collective-permute-start = (f32[2,4,4,8,8,128]{5,4,3,2,1,0:T(8,128)}, f32[2,4,4,8,8,128]{5,4,3,2,1,0:T(8,128)S(1)}, u32[]{:S(2)}, u32[]{:S(2)}) collective-permute-start(f32[2,4,4,8,8,128]{5,4,3,2,1,0:T(8,128)} %pad_maximum_fusion), channel_id=1, source_target_pairs={{0,16},{4,20},{8,24},{12,28},{16,0},{20,4},{24,8},{28,12},{1,17},{... | collective-permute-start | bytes 3145736 | tf_op jit(solution)/shard_map/ppermute | solution.py:12
  18.5 0.7 copy-done.4
  19.2 0.7 fusion.81
  19.9 44.5 %collective-permute-done = f32[2,4,4,8,8,128]{5,4,3,2,1,0:T(8,128)S(1)} collective-permute-done((f32[2,4,4,8,8,128]{5,4,3,2,1,0:T(8,128)}, f32[2,4,4,8,8,128]{5,4,3,2,1,0:T(8,128)S(1)}, u32[]{:S(2)}, u32[]{:S(2)}) %collective-permute-start) | collective-permute-done | bytes 1048608 | tf_op jit(solution)/shard_map/ppermute | solution.py:12
  64.5 2.8 %subtract_add_fusion = (f32[1,4,4,8,8,128]{5,4,3,2,1,0:T(8,128)S(1)}, f32[1,4,4,8,8,128]{5,4,3,2,1,0:T(8,128)S(1)}) fusion(f32[2,4,4,8,8,128]{5,4,3,2,1,0:T(8,128)S(1)} %get-tuple-element.10, f32[2,4,4,8,8,128]{5,4,3,2,1,0:T(8,128)S(1)} %get-tuple-element.9, f32[]{:T(128)} %bitcast.37, f32[]{:T(128)} %bitcast.36, f32[]{:T(128)} %bitcast.35, f32[]{:T(128)} %bitcast.34), kind=kLoop, calls=%fused_computation.41 | loop fusion | flops 1835008 | bytes 3145744 | tf_op jit(solution)/shard_map/add | solution.py:60
  67.3 2.7 %subtract_add_fusion.1 = (f32[1,4,4,8,8,128]{5,4,3,2,1,0:T(8,128)S(1)}, f32[1,4,4,8,8,128]{5,4,3,2,1,0:T(8,128)S(1)}) fusion(f32[2,4,4,8,8,128]{5,4,3,2,1,0:T(8,128)S(1)} %get-tuple-element.10, f32[2,4,4,8,8,128]{5,4,3,2,1,0:T(8,128)S(1)} %get-tuple-element.9, f32[]{:T(128)} %bitcast.33, f32[]{:T(128)} %bitcast.32, f32[]{:T(128)} %bitcast.31, f32[]{:T(128)} %bitcast), kind=kLoop, calls=%fused_computation.43 | loop fusion | flops 1835008 | bytes 3145744 | tf_op jit(solution)/shard_map/add | solution.py:60
  70.3 16.9 %all_to_all.5 = f32[2,4,4,8,8,128]{5,4,3,2,0,1:T(8,128)S(1)} all-to-all(f32[2,4,4,8,8,128]{5,4,3,2,0,1:T(8,128)S(1)} %copy.23), channel_id=1, replica_groups=mesh['grp'=8,'swap'=4] {'swap'}, dimensions={1} | all-to-all | bytes 2097152 | tf_op jit(solution)/shard_map/all_to_all | solution.py:100
  87.3 1.0 %fusion.12 = f32[1024,128]{1,0:T(8,128)S(1)} fusion(f32[16,8,8,128]{3,2,1,0:T(8,128)S(1)} %bitcast.180, f32[2,2,128,128]{3,2,1,0:T(8,128)S(1)} %copy-done.3), kind=kOutput, calls=%fused_computation.26 | convolution fusion | flops 201326592 | bytes 1114112 | tf_op jit(solution)/shard_map/dot_general | solution.py:49
  88.3 1.0 %fusion.8 = f32[1024,128]{1,0:T(8,128)S(1)} fusion(f32[16,8,8,128]{3,2,1,0:T(8,128)S(1)} %bitcast.184, f32[2,2,128,128]{3,2,1,0:T(8,128)S(1)} %copy-done.3), kind=kOutput, calls=%fused_computation.22 | convolution fusion | flops 201326592 | bytes 1114112 | tf_op jit(solution)/shard_map/dot_general | solution.py:52
  89.3 1.0 %fusion.3 = f32[128,1024]{0,1:T(8,128)S(1)} fusion(f32[1024,128]{1,0:T(8,128)S(1)} %fusion.12, f32[16,8,8,128]{3,2,1,0:T(8,128)S(1)} %bitcast.185, f32[2,2,128,128]{3,2,1,0:T(8,128)S(1)} %copy-done.3), kind=kOutput, calls=%fused_computation.7 | convolution fusion | flops 201457664 | bytes 1638400 | tf_op jit(solution)/shard_map/dot_general | solution.py:51
  91.2 1.0 %fusion.2 = f32[128,1024]{0,1:T(8,128)S(1)} fusion(f32[1024,128]{1,0:T(8,128)S(1)} %fusion.8, f32[16,8,8,128]{3,2,1,0:T(8,128)S(1)} %bitcast.181, f32[2,2,128,128]{3,2,1,0:T(8,128)S(1)} %copy-done.3), kind=kOutput, calls=%fused_computation.5 | convolution fusion | flops 201457664 | bytes 1638400 | tf_op jit(solution)/shard_map/dot_general | solution.py:54
  93.7 0.6 fusion
  94.3 1.1 %maximum_bitcast_fusion = f32[2,1,1,4,4,8,8,128]{7,6,5,4,3,2,1,0:T(8,128)} fusion(f32[1,4,4,8,8,128]{5,4,3,2,1,0:T(8,128)S(1)} %fusion, f32[1,4,4,8,8,128]{5,4,3,2,1,0:T(8,128)S(1)} %fusion.1), kind=kLoop, calls=%fused_computation.21 | loop fusion | flops 262144 | bytes 2097152 | tf_op jit(solution)/shard_map/broadcast_in_dim | solution.py:104
  (27 shorter events, 6.2 us)
Async XLA Ops:
  0.0 0.7 copy-start
  0.0 3.3 %copy-start.1 = (f32[2,1,1,4,4,8,8,128]{7,6,5,4,3,2,1,0:T(8,128)S(1)}, f32[2,1,1,4,4,8,8,128]{7,6,5,4,3,2,1,0:T(8,128)}, u32[]{:S(2)}) copy-start(f32[2,1,1,4,4,8,8,128]{7,6,5,4,3,2,1,0:T(8,128)} %param.6) | copy-start | bytes 3145732
  3.3 1.5 %copy-start.2 = (f32[3,2,128,128]{3,2,1,0:T(8,128)S(1)}, f32[3,2,128,128]{3,2,1,0:T(8,128)}, u32[]{:S(2)}) copy-start(f32[3,2,128,128]{3,2,1,0:T(8,128)} %param.7) | copy-start | bytes 1179652
  5.5 1.0 copy-start.3
  14.4 49.9 %collective-permute-start = (f32[2,4,4,8,8,128]{5,4,3,2,1,0:T(8,128)}, f32[2,4,4,8,8,128]{5,4,3,2,1,0:T(8,128)S(1)}, u32[]{:S(2)}, u32[]{:S(2)}) collective-permute-start(f32[2,4,4,8,8,128]{5,4,3,2,1,0:T(8,128)} %pad_maximum_fusion), channel_id=1, source_target_pairs={{0,16},{4,20},{8,24},{12,28},{16,0},{20,4},{24,8},{28,12},{1,17},{... | collective-permute-start | bytes 3145736 | tf_op jit(solution)/shard_map/ppermute | solution.py:12
  18.5 0.7 copy-start.4
where the time goes:
time: 95.7 us; the launch traced here: 95.3 us
  waiting for transfers between devices  44.5 us (46%)
  matrix products  17.9 us (19%)
  blocking collectives  16.9 us (18%)
  other arithmetic  7.94 us (8%)
  starting transfers between devices  4.06 us (4%)
  local copies, waits for them, and re-layouts  3.76 us (4%)
    ppermute x1, waiting for transfers between devices, swapped(): return lax.ppermute(value, axis, pairs)  44.5 us
    all_to_all x1, blocking collectives, local(): lax.all_to_all(current, 'swap', split_axis=1, concat_axis=1, tiled=True)  16.9 us
    add x2, other arithmetic, apply_row(): pair_gate[0, target, 0] * lower[0] - pair_gate[1, target, 0] * lower[1]  5.46 us
    ppermute x1, starting transfers between devices, swapped(): return lax.ppermute(value, axis, pairs)  4.06 us
    dot_general x3, matrix products, low_gate(): jnp.einsum('...k,ik->...i', psi_block[0], matrix[0], precision=highest, p...  2.95 us
    dot_general x3, matrix products, low_gate(): jnp.einsum('...k,ik->...i', psi_block[1], matrix[0], precision=highest, p...  2.66 us
    unnamed x14, local copies, waits for them, and re-layouts  2.13 us
    dot_general x2, matrix products, mid_gate(): jnp.dot(matrix[1], flat[1], precision=highest, preferred_element_type=jnp...  2 us
  transfers between devices with their start and end apart: 1, of which 1 were waited for; matrix products, arithmetic and copies ran while one was open for 1% of the time, Pallas kernels for 0%

commit v1 on v0

v1 whole, which is shorter than its diff:
```python
import functools

import jax
import jax.numpy as jnp
from jax import lax
from jax.experimental import pallas as pl
from jax.experimental.pallas import tpu as pltpu
from jax.sharding import PartitionSpec as P

MESH = pl.DeviceIdType.MESH
highest = lax.Precision.HIGHEST


def dot(a, b):
    return jnp.dot(a, b, precision=highest, preferred_element_type=jnp.float32)


def dot_nt(a, b):
    return lax.dot_general(
        a, b, (((1,), (1,)), ((), ())), precision=highest, preferred_element_type=jnp.float32
    )


def embedded(re, im):
    return jnp.concatenate(
        [jnp.concatenate([re, -im], axis=1), jnp.concatenate([im, re], axis=1)], axis=0
    )


def mixed(own, other, own_re, own_im, other_re, other_im):
    re = (own[0] * own_re - own[1] * own_im) + (other[0] * other_re - other[1] * other_im)
    im = (own[0] * own_im + own[1] * own_re) + (other[0] * other_im + other[1] * other_re)
    return re, im


def kernel(
    dims,
    x_ref, low_ref, mid_ref, pair_ref, bits_ref, angle_ref,
    out_ref,
    x_v, low_v, mid_v, angle_v, out_v,
    early_x, early_rx, early_y, early_t, late_y, late_t, late_z, late_rz,
    load_sem, ze_send, ze_recv, zl_send, zl_recv, ae_send, ae_recv, al_send, al_recv, store_sem,
):
    groups, swaps, m_size, rows, low, early, blocks = dims
    late = rows - early
    part = m_size // swaps
    piece = m_size // blocks
    grp = lax.axis_index("grp")
    me = lax.axis_index("swap")
    half = groups // 2
    top = grp // half
    partner = (grp + half) % groups

    barrier = pltpu.get_barrier_semaphore()
    pl.semaphore_signal(barrier, inc=1, device_id={"grp": partner}, device_id_type=MESH)
    for d in range(1, swaps):
        pl.semaphore_signal(
            barrier, inc=1, device_id={"swap": lax.bitwise_xor(me, d)}, device_id_type=MESH
        )
    loads = [
        pltpu.make_async_copy(src, dst, load_sem.at[i])
        for i, (src, dst) in enumerate(
            [(x_ref, x_v), (low_ref, low_v), (mid_ref, mid_v), (angle_ref, angle_v)]
        )
    ]
    for load in loads:
        load.start()
    loads[0].wait()

    def x_row(c, r):
        return x_v[pl.ds(c * m_size * rows + r, m_size, stride=rows), :]

    for r in range(early):
        for c in range(2):
            early_x[r, c] = x_row(c, r)
    pl.semaphore_wait(barrier, swaps)

    raw = [
        pltpu.make_async_remote_copy(
            src_ref=early_x.at[r], dst_ref=early_rx.at[r],
            send_sem=ze_send.at[r], recv_sem=ze_recv.at[r],
            device_id={"grp": partner}, device_id_type=MESH,
        )
        for r in range(early)
    ]
    for copy in raw:
        copy.start()

    for load in loads[1:]:
        load.wait()
    theta = bits_ref[0].astype(jnp.float32) * angle_v[0:1, :]
    for j in range(1, angle_v.shape[0]):
        theta = theta + bits_ref[j].astype(jnp.float32) * angle_v[j : j + 1, :]
    cosine, sine = jnp.cos(theta), jnp.sin(theta)
    w = jnp.concatenate([low_v[0, 0], low_v[0, 1]], axis=0)
    for i in range(1, low_v.shape[0]):
        w = dot(embedded(low_v[i, 0], low_v[i, 1]), w)
    w_re, w_im = w[:low], w[low:]
    w = embedded(w_re * cosine - w_im * sine, w_re * sine + w_im * cosine)
    mid_first = embedded(mid_v[0, 0], mid_v[0, 1])
    mid_second = embedded(mid_v[1, 0], mid_v[1, 1])

    def first_gates(pairs, y_ref):
        for i, (re, im) in enumerate(pairs):
            y = dot_nt(jnp.concatenate([re, im], axis=1), w)
            y = dot(mid_first, jnp.concatenate([y[:, :low], y[:, low:]], axis=0))
            y_ref[i, 0] = y[:m_size]
            y_ref[i, 1] = y[m_size:]

    def trade(y_ref, t_ref, send, recv):
        mine = pl.ds(pl.multiple_of(me * part, part), part)
        copies = []
        for d in range(1, swaps):
            to = lax.bitwise_xor(me, d)
            copy = pltpu.make_async_remote_copy(
                src_ref=y_ref.at[:, :, pl.ds(pl.multiple_of(to * part, part), part), :],
                dst_ref=t_ref.at[:, :, mine, :],
                send_sem=send.at[d], recv_sem=recv.at[d],
                device_id={"swap": to}, device_id_type=MESH,
            )
            copy.start()
            copies.append(copy)
        t_ref[:, :, mine, :] = y_ref[:, :, mine, :]
        for copy in copies:
            copy.wait()

    def last_gate(t_ref, i):
        z = dot(mid_second, jnp.concatenate([t_ref[i, 0], t_ref[i, 1]], axis=0))
        return z[:m_size], z[m_size:]

    own_re, own_im = pair_ref[0, top, top], pair_ref[1, top, top]
    other_re, other_im = pair_ref[0, top, 1 - top], pair_ref[1, top, 1 - top]

    first_gates([(x_row(0, r), x_row(1, r)) for r in range(early, rows)], late_y)
    trade(late_y, late_t, al_send, al_recv)
    for i in range(late):
        z_re, z_im = last_gate(late_t, i)
        late_z[i, 0] = z_re
        late_z[i, 1] = z_im
    finished = []
    for k in range(blocks):
        rows_k = pl.ds(k * piece, piece)
        copy = pltpu.make_async_remote_copy(
            src_ref=late_z.at[:, :, rows_k, :], dst_ref=late_rz.at[:, :, rows_k, :],
            send_sem=zl_send.at[k], recv_sem=zl_recv.at[k],
            device_id={"grp": partner}, device_id_type=MESH,
        )
        copy.start()
        finished.append(copy)

    for copy in raw:
        copy.wait()
    first_gates(
        [
            mixed(
                (early_x[r, 0], early_x[r, 1]), (early_rx[r, 0], early_rx[r, 1]),
                own_re, own_im, other_re, other_im,
            )
            for r in range(early)
        ],
        early_y,
    )
    trade(early_y, early_t, ae_send, ae_recv)
    for r in range(early):
        for c, value in enumerate(last_gate(early_t, r)):
            out_v[pl.ds(c * m_size * rows + r, m_size, stride=rows), :] = value

    stores = []
    for k in range(blocks):
        finished[k].wait_recv()
        at = slice(k * piece, (k + 1) * piece)
        for i in range(late):
            pair = mixed(
                (late_z[i, 0, at], late_z[i, 1, at]), (late_rz[i, 0, at], late_rz[i, 1, at]),
                own_re, own_im, other_re, other_im,
            )
            for c in range(2):
                start = (c * m_size + k * piece) * rows + early + i
                out_v[pl.ds(start, piece, stride=rows), :] = pair[c]
        for c in range(2):
            span = pl.ds((c * m_size + k * piece) * rows, piece * rows)
            store = pltpu.make_async_copy(out_v.at[span], out_ref.at[span], store_sem.at[2 * k + c])
            store.start()
            stores.append(store)
    for copy in finished:
        copy.wait_send()
    for store in stores:
        store.wait()


def local(groups, swaps, amplitudes, low_gates, mid_gates, pair_gate, slice_bits, phase_angles):
    _, _, _, a_size, b_size, q_size, rows, low = amplitudes.shape
    m_size = a_size * b_size * q_size
    early = max(1, rows * 3 // 8)
    late = rows - early
    blocks = 8
    flat = amplitudes.reshape(2 * m_size * rows, low)
    f32 = jnp.float32
    dma = pltpu.SemaphoreType.DMA
    anywhere = pl.BlockSpec(memory_space=pl.ANY)
    scalars = pl.BlockSpec(memory_space=pltpu.SMEM)
    out = pl.pallas_call(
        functools.partial(kernel, (groups, swaps, m_size, rows, low, early, blocks)),
        out_shape=jax.ShapeDtypeStruct(flat.shape, f32),
        in_specs=[anywhere, anywhere, anywhere, scalars, scalars, anywhere],
        out_specs=anywhere,
        scratch_shapes=[
            pltpu.VMEM(flat.shape, f32),
            pltpu.VMEM(low_gates.shape, f32),
            pltpu.VMEM(mid_gates.shape, f32),
            pltpu.VMEM(phase_angles.shape, f32),
            pltpu.VMEM(flat.shape, f32),
        ]
        + [pltpu.VMEM((early, 2, m_size, low), f32)] * 4
        + [pltpu.VMEM((late, 2, m_size, low), f32)] * 4
        + [
            dma((4,)),
            dma((early,)), dma((early,)),
            dma((blocks,)), dma((blocks,)),
            dma((swaps,)), dma((swaps,)), dma((swaps,)), dma((swaps,)),
            dma((2 * blocks,)),
        ],
        compiler_params=pltpu.CompilerParams(collective_id=0, has_side_effects=True),
        name="evolve",
    )(flat, low_gates, mid_gates, pair_gate, slice_bits, phase_angles)
    return out.reshape(amplitudes.shape)


def solution(mesh):
    spec = P(None, "grp", "swap", None, None, None, None, None)
    return jax.shard_map(
        functools.partial(local, mesh.shape["grp"], mesh.shape["swap"]),
        mesh=mesh,
        in_specs=(spec, P(), P(), P(), P(), P()),
        out_specs=spec,
        check_vma=False,
    )
```

time: 95.7 us -> 56.3 us (0.59)
  Pallas kernels: 0 us -> 53.8 us
  waiting for transfers between devices: 44.5 us -> 0 us
  matrix products: 17.9 us -> 0 us
  blocking collectives: 16.9 us -> 0 us
  other arithmetic: 7.94 us -> 0 us
  starting transfers between devices: 4.06 us -> 0 us
  local copies, waits for them, and re-layouts: 3.76 us -> 2.31 us
    pallas_call x0 -> x1, Pallas kernels: none -> 53.8 us  [local(): pl.pallas_call(functools.partial(kernel, (groups, swaps, m_size, rows, lo...]
    ppermute x1 -> x0, waiting for transfers between devices: 44.5 us -> none  [swapped(): return lax.ppermute(value, axis, pairs)]
    dot_general x21 -> x0, matrix products: 17.9 us -> none  [the longest x3 2.95 us: low_gate(): jnp.einsum('...k,ik->...i', psi_block[0], matrix[0], precision=highest, p...]
    all_to_all x1 -> x0, blocking collectives: 16.9 us -> none  [local(): lax.all_to_all(current, 'swap', split_axis=1, concat_axis=1, tiled=True)]
    add x2 -> x0, other arithmetic: 5.46 us -> none  [apply_row(): pair_gate[0, target, 0] * lower[0] - pair_gate[1, target, 0] * lower[1]]
    ppermute x1 -> x0, starting transfers between devices: 4.06 us -> none  [swapped(): return lax.ppermute(value, axis, pairs)]
    broadcast_in_dim x1 -> x0, other arithmetic: 1.06 us -> none  [local(): return current[:, None, None]]
    another operation x1 -> x0, other arithmetic: 1.04 us -> none  [low_gate(): return jnp.stack([real_part, imag_part])]
  transfers between devices with their start and end apart: 1 -> 0, of which waited for: 1 -> 0; matrix products, arithmetic and copies ran while one was open for 1% -> 0% of each run, Pallas kernels for 0% -> 0%
where the time goes in v1:
time: 56.3 us; the launch traced here: 56.1 us
  Pallas kernels  53.8 us (96%)
  local copies, waits for them, and re-layouts  2.31 us (4%)
    pallas_call x1, Pallas kernels, local(): pl.pallas_call(functools.partial(kernel, (groups, swaps, m_size, rows, lo...  53.8 us
    unnamed x1, local copies, waits for them, and re-layouts  2.31 us

profile of v1, /device:TPU:0, one launch (start us, length us, event | category | flops | bytes accessed | tf_op | source)
XLA Modules:
  0.0 56.1 jit_solution(5962623124500980791)
XLA Ops:
  0.0 53.8 %evolve.1 = f32[2048,128]{1,0:T(8,128)} custom-call(f32[2048,128]{1,0:T(8,128)} %bitcast.5, f32[3,2,128,128]{3,2,1,0:T(8,128)} %low_ref.1, f32[2,2,128,128]{3,2,1,0:T(8,128)} %mid_ref.1, f32[2,2,2]{2,1,0:T(2,128)} %pair_ref.1, s32[13]{0:T(128)} %bits_ref.1, f32[13,128]{1,0:T(8,128)} %angle_ref.1), custom_call_target="tpu_custom_call" | custom-call | tf_op jit(solution)/shard_map/evolve/pallas_call | solution.py:202
  53.8 2.3 %copy.9 = f32[2,1,1,4,4,8,8,128]{7,6,5,4,3,2,1,0:T(8,128)} copy(f32[2,1,1,4,4,8,8,128]{7,6,5,4,3,2,1,0:T(8,128)} %bitcast.4) | data formatting | bytes 2097152

commit v2 on v1

--- a/solution.py
+++ b/solution.py
@@ -39,7 +39,7 @@
     out_ref,
     x_v, low_v, mid_v, angle_v, out_v,
     early_x, early_rx, early_y, early_t, late_y, late_t, late_z, late_rz,
-    load_sem, ze_send, ze_recv, zl_send, zl_recv, ae_send, ae_recv, al_send, al_recv, store_sem,
+    load_sem, ze_send, ze_recv, zl_send, zl_recv, ae_send, ae_recv, al_send, al_recv, store_sem, gate_sem,
 ):
     groups, swaps, m_size, rows, low, early, blocks = dims
     late = rows - early
@@ -50,9 +50,18 @@
     half = groups // 2
     top = grp // half
     partner = (grp + half) % groups
+    quarter = half // 2
+    gated = quarter > 0
+    if gated:
+        outer = (grp % half) // quarter
+        mate = grp + quarter - 2 * quarter * outer
+        holds = jnp.logical_and(top == 1, outer == 1)
+        frees = jnp.logical_and(top == 1, outer == 0)
 
     barrier = pltpu.get_barrier_semaphore()
     pl.semaphore_signal(barrier, inc=1, device_id={"grp": partner}, device_id_type=MESH)
+    if gated:
+        pl.semaphore_signal(barrier, inc=1, device_id={"grp": mate}, device_id_type=MESH)
     for d in range(1, swaps):
         pl.semaphore_signal(
             barrier, inc=1, device_id={"swap": lax.bitwise_xor(me, d)}, device_id_type=MESH
@@ -73,7 +82,7 @@
     for r in range(early):
         for c in range(2):
             early_x[r, c] = x_row(c, r)
-    pl.semaphore_wait(barrier, swaps)
+    pl.semaphore_wait(barrier, swaps + 1 if gated else swaps)
 
     raw = [
         pltpu.make_async_remote_copy(
@@ -145,7 +154,10 @@
             send_sem=zl_send.at[k], recv_sem=zl_recv.at[k],
             device_id={"grp": partner}, device_id_type=MESH,
         )
-        copy.start()
+        if gated and k == blocks - 1:
+            pl.when(jnp.logical_not(holds))(copy.start)
+        else:
+            copy.start()
         finished.append(copy)
 
     for copy in raw:
@@ -182,8 +194,20 @@
             store = pltpu.make_async_copy(out_v.at[span], out_ref.at[span], store_sem.at[2 * k + c])
             store.start()
             stores.append(store)
-    for copy in finished:
-        copy.wait_send()
+        if gated and k == blocks - 3:
+            finished[blocks - 2].wait_send()
+
+            @pl.when(frees)
+            def _():
+                pl.semaphore_signal(gate_sem, inc=1, device_id={"grp": mate}, device_id_type=MESH)
+
+            @pl.when(holds)
+            def _():
+                pl.semaphore_wait(gate_sem, 1)
+                finished[blocks - 1].start()
+    for k in range(blocks):
+        if not gated or k != blocks - 2:
+            finished[k].wait_send()
     for store in stores:
         store.wait()
 
@@ -219,6 +243,7 @@
             dma((blocks,)), dma((blocks,)),
             dma((swaps,)), dma((swaps,)), dma((swaps,)), dma((swaps,)),
             dma((2 * blocks,)),
+            pltpu.SemaphoreType.REGULAR,
         ],
         compiler_params=pltpu.CompilerParams(collective_id=0, has_side_effects=True),
         name="evolve",

time: 56.3 us -> 54.6 us (0.970)
  Pallas kernels: 53.8 us -> 52.1 us
    pallas_call x1, Pallas kernels: 53.8 us -> 52.1 us  [local(): pl.pallas_call(functools.partial(kernel, (groups, swaps, m_size, rows, lo...]
where the time goes in v2:
time: 54.6 us; the launch traced here: 54.4 us
  Pallas kernels  52.1 us (95%)
  local copies, waits for them, and re-layouts  2.31 us (4%)
    pallas_call x1, Pallas kernels, local(): pl.pallas_call(functools.partial(kernel, (groups, swaps, m_size, rows, lo...  52.1 us
    unnamed x1, local copies, waits for them, and re-layouts  2.31 us

profile of v2, /device:TPU:0, one launch (start us, length us, event | category | flops | bytes accessed | tf_op | source)
XLA Modules:
  0.0 54.4 jit_solution(14346871380826518091)
XLA Ops:
  0.0 52.1 %evolve.1 = f32[2048,128]{1,0:T(8,128)} custom-call(f32[2048,128]{1,0:T(8,128)} %bitcast.5, f32[3,2,128,128]{3,2,1,0:T(8,128)} %low_ref.1, f32[2,2,128,128]{3,2,1,0:T(8,128)} %mid_ref.1, f32[2,2,2]{2,1,0:T(2,128)} %pair_ref.1, s32[13]{0:T(128)} %bits_ref.1, f32[13,128]{1,0:T(8,128)} %angle_ref.1), custom_call_target="tpu_custom_call" | custom-call | tf_op jit(solution)/shard_map/evolve/pallas_call | solution.py:226
  52.1 2.3 %copy.9 = f32[2,1,1,4,4,8,8,128]{7,6,5,4,3,2,1,0:T(8,128)} copy(f32[2,1,1,4,4,8,8,128]{7,6,5,4,3,2,1,0:T(8,128)} %bitcast.4) | data formatting | bytes 2097152

commit v3 on v1

--- a/solution.py
+++ b/solution.py
@@ -35,13 +35,13 @@
 
 def kernel(
     dims,
-    x_ref, low_ref, mid_ref, pair_ref, bits_ref, angle_ref,
+    x_ref, low_ref, mid_ref, pair_in, bits_in, angle_ref,
     out_ref,
-    x_v, low_v, mid_v, angle_v, out_v,
+    x_v, low_v, mid_v, angle_v, pair_ref, bits_ref, out_v,
     early_x, early_rx, early_y, early_t, late_y, late_t, late_z, late_rz,
-    load_sem, ze_send, ze_recv, zl_send, zl_recv, ae_send, ae_recv, al_send, al_recv, store_sem,
+    x_sem, load_sem, ze_send, ze_recv, zl_send, zl_recv, ae_send, ae_recv, al_send, al_recv, store_sem,
 ):
-    groups, swaps, m_size, rows, low, early, blocks = dims
+    groups, swaps, m_size, rows, low, early, blocks, pieces = dims
     late = rows - early
     part = m_size // swaps
     piece = m_size // blocks
@@ -50,6 +50,7 @@
     half = groups // 2
     top = grp // half
     partner = (grp + half) % groups
+    holds = 4 * grp >= 3 * groups
 
     barrier = pltpu.get_barrier_semaphore()
     pl.semaphore_signal(barrier, inc=1, device_id={"grp": partner}, device_id_type=MESH)
@@ -57,36 +58,51 @@
         pl.semaphore_signal(
             barrier, inc=1, device_id={"swap": lax.bitwise_xor(me, d)}, device_id_type=MESH
         )
+    span = m_size // pieces
+    x_loads = []
+    for j in range(pieces):
+        for c in range(2):
+            at = pl.ds((c * m_size + j * span) * rows, span * rows)
+            x_loads.append(
+                pltpu.make_async_copy(x_ref.at[at], x_v.at[at], x_sem.at[2 * j + c])
+            )
     loads = [
         pltpu.make_async_copy(src, dst, load_sem.at[i])
-        for i, (src, dst) in enumerate(
-            [(x_ref, x_v), (low_ref, low_v), (mid_ref, mid_v), (angle_ref, angle_v)]
-        )
+        for i, (src, dst) in enumerate([(low_ref, low_v), (mid_ref, mid_v), (angle_ref, angle_v), (pair_in, pair_ref), (bits_in, bits_ref)])
     ]
-    for load in loads:
+    for load in x_loads + loads:
         load.start()
-    loads[0].wait()
 
     def x_row(c, r):
         return x_v[pl.ds(c * m_size * rows + r, m_size, stride=rows), :]
 
-    for r in range(early):
+    def gather(j):
         for c in range(2):
-            early_x[r, c] = x_row(c, r)
+            x_loads[2 * j + c].wait()
+        for r in range(early):
+            for c in range(2):
+                start = (c * m_size + j * span) * rows + r
+                early_x[r, c, j * span : (j + 1) * span, :] = x_v[pl.ds(start, span, stride=rows), :]
+
+    raw = []
+    for j in range(pieces):
+        at = pl.ds(j * span, span)
+        raw.append(
+            pltpu.make_async_remote_copy(
+                src_ref=early_x.at[:, :, at, :], dst_ref=early_rx.at[:, :, at, :],
+                send_sem=ze_send.at[j], recv_sem=ze_recv.at[j],
+                device_id={"grp": partner}, device_id_type=MESH,
+            )
+        )
+    gather(0)
+    gather(1)
     pl.semaphore_wait(barrier, swaps)
-
-    raw = [
-        pltpu.make_async_remote_copy(
-            src_ref=early_x.at[r], dst_ref=early_rx.at[r],
-            send_sem=ze_send.at[r], recv_sem=ze_recv.at[r],
-            device_id={"grp": partner}, device_id_type=MESH,
-        )
-        for r in range(early)
-    ]
-    for copy in raw:
-        copy.start()
-
-    for load in loads[1:]:
+    for j in range(pieces):
+        raw[j].start()
+        if j + 2 < pieces:
+            gather(j + 2)
+
+    for load in loads:
         load.wait()
     theta = bits_ref[0].astype(jnp.float32) * angle_v[0:1, :]
     for j in range(1, angle_v.shape[0]):
@@ -145,7 +161,10 @@
             send_sem=zl_send.at[k], recv_sem=zl_recv.at[k],
             device_id={"grp": partner}, device_id_type=MESH,
         )
-        copy.start()
+        if k == blocks - 1:
+            pl.when(jnp.logical_not(holds))(copy.start)
+        else:
+            copy.start()
         finished.append(copy)
 
     for copy in raw:
@@ -182,6 +201,8 @@
             store = pltpu.make_async_copy(out_v.at[span], out_ref.at[span], store_sem.at[2 * k + c])
             store.start()
             stores.append(store)
+        if k == blocks - 3:
+            pl.when(holds)(finished[blocks - 1].start)
     for copy in finished:
         copy.wait_send()
     for store in stores:
@@ -193,36 +214,43 @@
     m_size = a_size * b_size * q_size
     early = max(1, rows * 3 // 8)
     late = rows - early
-    blocks = 8
+    blocks, pieces = 8, 4
     flat = amplitudes.reshape(2 * m_size * rows, low)
     f32 = jnp.float32
     dma = pltpu.SemaphoreType.DMA
     anywhere = pl.BlockSpec(memory_space=pl.ANY)
-    scalars = pl.BlockSpec(memory_space=pltpu.SMEM)
+    in_hbm = [
+        pltpu.with_memory_space_constraint(value, pltpu.HBM)
+        for value in (flat, low_gates, mid_gates, pair_gate, slice_bits, phase_angles)
+    ]
     out = pl.pallas_call(
-        functools.partial(kernel, (groups, swaps, m_size, rows, low, early, blocks)),
+        functools.partial(kernel, (groups, swaps, m_size, rows, low, early, blocks, pieces)),
         out_shape=jax.ShapeDtypeStruct(flat.shape, f32),
-        in_specs=[anywhere, anywhere, anywhere, scalars, scalars, anywhere],
+        in_specs=[anywhere] * 6,
         out_specs=anywhere,
         scratch_shapes=[
             pltpu.VMEM(flat.shape, f32),
             pltpu.VMEM(low_gates.shape, f32),
             pltpu.VMEM(mid_gates.shape, f32),
             pltpu.VMEM(phase_angles.shape, f32),
+            pltpu.SMEM(pair_gate.shape, f32),
+            pltpu.SMEM(slice_bits.shape, jnp.int32),
             pltpu.VMEM(flat.shape, f32),
         ]
         + [pltpu.VMEM((early, 2, m_size, low), f32)] * 4
         + [pltpu.VMEM((late, 2, m_size, low), f32)] * 4
         + [
-            dma((4,)),
-            dma((early,)), dma((early,)),
+            dma((2 * pieces,)), dma((5,)),
+            dma((pieces,)), dma((pieces,)),
             dma((blocks,)), dma((blocks,)),
             dma((swaps,)), dma((swaps,)), dma((swaps,)), dma((swaps,)),
             dma((2 * blocks,)),
         ],
-        compiler_params=pltpu.CompilerParams(collective_id=0, has_side_effects=True),
+        compiler_params=pltpu.CompilerParams(
+            collective_id=0, has_side_effects=True, vmem_limit_bytes=24 << 20
+        ),
         name="evolve",
-    )(flat, low_gates, mid_gates, pair_gate, slice_bits, phase_angles)
+    )(*in_hbm)
     return out.reshape(amplitudes.shape)
 
 

time: 56.3 us -> 52.9 us (0.940); the launches traced: 56.1 us -> 52 us
  Pallas kernels: 53.8 us -> 51 us
  local copies, waits for them, and re-layouts: 2.31 us -> 0.97 us
    pallas_call x1, Pallas kernels: 53.8 us -> 51 us  [local(): pl.pallas_call(functools.partial(kernel, (groups, swaps, m_size, rows, lo...]
    unnamed x1, local copies, waits for them, and re-layouts: 2.31 us -> 0.97 us
where the time goes in v3:
time: 52.9 us; the launch traced here: 52 us
  Pallas kernels  51 us (96%)
  local copies, waits for them, and re-layouts  0.97 us (2%)
    pallas_call x1, Pallas kernels, local(): pl.pallas_call(functools.partial(kernel, (groups, swaps, m_size, rows, lo...  51 us

profile of v3, /device:TPU:0, one launch (start us, length us, event | category | flops | bytes accessed | tf_op | source)
XLA Modules:
  0.0 52.0 jit_solution(6452216249062971026)
XLA Ops:
  0.0 51.0 %evolve.1 = f32[2048,128]{1,0:T(8,128)S(1)} custom-call(f32[2048,128]{1,0:T(8,128)} %bitcast.5, f32[3,2,128,128]{3,2,1,0:T(8,128)} %low_ref.1, f32[2,2,128,128]{3,2,1,0:T(8,128)} %mid_ref.1, f32[2,2,2]{2,1,0:T(2,128)} %pair_in.1, s32[13]{0:T(128)} %bits_in.1, f32[13,128]{1,0:T(8,128)} %angle_ref.1), custom_call_target="tpu_custom_call" | custom-call | tf_op jit(solution)/shard_map/evolve/pallas_call | solution.py:226
  51.0 1.0 %copy.9 = f32[2,1,1,4,4,8,8,128]{7,6,5,4,3,2,1,0:T(8,128)} copy(f32[2,1,1,4,4,8,8,128]{7,6,5,4,3,2,1,0:T(8,128)S(1)} %bitcast.4) | data formatting | bytes 2097152
